TPU v7x, 256 devices: a whole 4x4x8 slice. The times are simulated.
256 devices in a mesh: gx: 32 (over y, x, core), gy: 8 (over z).
Axes of the slice: x: 4, y: 4, z: 8, core: 2. Of those that a mesh axis runs over, the one named last changes fastest.
Arguments:
- velocity: float32 [2, 10, 3072, 3072], P(None, None, 'gx', 'gy'), may hold values from -6 to 6
- viscosity: float32 [10, 3072, 3072], P(None, 'gx', 'gy'), may hold values from 0.05 to 0.8
- friction: float32 [3072, 3072], P('gx', 'gy'), may hold values from 0.1 to 2
- ice_mask: int32 [32, 8], P('gx', 'gy'), may hold values from 0 to 1, as said below
- obs_tiles: float32 [32, 8, 32, 8, 4, 3, 128], P('gx', 'gy'), as said below
- obs_cell: int32 [32, 8, 32, 8, 4], P('gx', 'gy'), may hold values from 0 to 287, as said below
- obs_count: int32 [32, 8, 32, 8], P('gx', 'gy'), may hold values from 0 to 4, as said below
Outputs:
- adjoint: float32 [2, 10, 3072, 3072], P(None, None, 'gx', 'gy')
- friction_gradient: float32 [3072, 3072], P('gx', 'gy')
Inputs may be any that keep to these rules, and one draw needn't show every extreme that they name: `ice_mask`: some block is ice-covered in every draw. `obs_count`: zero for every owner block whose ice_mask is 0; in every draw some owner block receives 4 live tiles from every sending block. `obs_cell`: slots at or beyond the live count also hold anchors in range. `obs_tiles`: channel 2 holds weights between 0.3 and 3.
All inputs are finite; a program needn't handle non-finite values.
Results may differ from a plain program's by a relative error of at most 0.00002.
Values sent between devices are 32-bit elements; how exact they have to be, the bound alone decides.
A program may use at most 128 MiB of HBM per device.

v0:
```python
import functools

import jax
import jax.numpy as jnp
from jax import lax
from jax.experimental import pallas as pl
from jax.experimental.pallas import tpu as pltpu
from jax.sharding import PartitionSpec as P

MESH = pl.DeviceIdType.MESH
RELAX = 0.8
LANES = 128
HALO = 8
F32 = jnp.float32


def shifts(nb, lane, values, low_halo, high_halo):
    ups = [low_halo] + [pltpu.roll(a, 1, 1) for a in values]
    downs = [pltpu.roll(a, LANES - 1, 1) for a in values] + [high_halo]
    low = [jnp.where(lane == 0, ups[t], ups[t + 1]) for t in range(nb)]
    high = [jnp.where(lane == LANES - 1, downs[t + 1], downs[t]) for t in range(nb)]
    return low, high


def at(i, shift=0):
    return pl.ds(pl.multiple_of(i * 8, 8) + HALO + shift, 8)


def plain(i):
    return pl.ds(pl.multiple_of(i * 8, 8), 8)


def halo_cols(packed, i, q, exists):
    lo = pltpu.roll(packed[0, plain(i), :], (LANES - q) % LANES, 1) * exists[0]
    hi = pltpu.roll(packed[1, plain(i), :], LANES - 1 - q, 1) * exists[1]
    return lo, hi


def put(packed, lane, q, value, edge):
    return jnp.where(lane == q, pltpu.roll(value, (q - edge) % LANES, 1), packed)


def solve(i, c, lane, nb, old, cols, exists, faces, carry_c, ratio_c, rhs, keep, gain, emit):
    west, east, south, north = faces
    layers, r = west.shape[0], plain(i)
    forward = []
    for k in range(layers):
        centre = [old[c, k, t, at(i), :] for t in range(nb)]
        low, high = shifts(nb, lane, centre, *halo_cols(cols, i, c * layers + k, exists))
        level = []
        for t in range(nb):
            value = west[k, t, r, :] * old[c, k, t, at(i, -1), :] + east[k, t, r, :] * old[c, k, t, at(i, 1), :]
            value = value + (south[k, t, r, :] * low[t] + north[k, t, r, :] * high[t])
            if k > 0:
                value = value + carry_c[k - 1, t, r, :] * forward[k - 1][t]
            if k == layers - 1:
                value = value + rhs[c, t, r, :]
            level.append(value)
        forward.append(level)
    x = forward[layers - 1]
    for k in range(layers - 1, -1, -1):
        if k < layers - 1:
            x = [forward[k][t] + ratio_c[k, t, r, :] * x[t] for t in range(nb)]
        emit(k, [keep * old[c, k, t, at(i), :] + gain * x[t] for t in range(nb)])


def gather_and_sweep(nx, ny, width, staged, tiles, cell, count, velocity, viscosity, friction, ice,
                     adj_b, west, east, south, north, carry_c, ratio_c, rhs, cols_b,
                     eta, adj_a, top_c, vel, fric, cell_v, count_v, mid, got, row_out, row_in, block, anchors, lookup, total,
                     row_s, row_r, col_s, col_r,
                     load_sem, send_sem, recv_sem, entered, z_send, z_recv, own, far_send, far_recv, near_send, near_recv,
                     small_send, small_recv):
    sx, sy = lax.axis_index("gx"), lax.axis_index("gy")
    layers, nb, rows = west.shape[0], west.shape[1], west.shape[2]
    slots, groups, blocks = cell_v.shape[1], nx // width, rows // 8

    def x_at(d):
        return lax.rem(sx + d, nx)

    def y_at(d):
        return lax.rem(sy + d, ny)

    barrier = pltpu.get_barrier_semaphore()
    for d in range(1, ny):
        pl.semaphore_signal(barrier, inc=1, device_id=(sx, y_at(d)), device_id_type=MESH)

    def greet(d, carry):
        pl.semaphore_signal(barrier, inc=1, device_id=(x_at(d), sy), device_id_type=MESH)
        return carry

    lax.fori_loop(1, nx, greet, 0)

    loads = [pltpu.make_async_copy(cell, cell_v, load_sem.at[0]), pltpu.make_async_copy(count, count_v, load_sem.at[1])]
    for t in range(nb):
        part = pl.ds(t * LANES, LANES)
        loads.append(pltpu.make_async_copy(viscosity.at[:, :, part], eta.at[:, t, pl.ds(HALO, rows), :], load_sem.at[2 + t]))
    loads.append(pltpu.make_async_copy(friction, fric, load_sem.at[2 + nb]))
    for c in range(2):
        loads.append(pltpu.make_async_copy(velocity.at[c, layers - 1], vel.at[c], load_sem.at[3 + nb + c]))
    kept = pltpu.make_async_copy(tiles.at[:, sy], mid.at[:, sy], own.at[0])
    for load in loads:
        load.start()
    kept.start()

    row_out[...] = jnp.full(row_out.shape, -1, jnp.int32)
    for load in loads[:2]:
        load.wait()
    for oy in range(ny):
        slot = lax.broadcasted_iota(jnp.int32, (slots, nx), 0)
        live = jnp.where(slot < count_v[oy : oy + 1, :], cell_v[oy], -1)
        for s in range(slots):
            row_out[oy, :, s * nx : (s + 1) * nx] = live[s : s + 1, :]

    pl.semaphore_wait(barrier, nx + ny - 2)

    for d in range(1, ny):
        pl.semaphore_signal(entered, inc=1, device_id=(sx, y_at(d)), device_id_type=MESH)

    def group(g):
        return lax.rem(sx // width + g, groups) * width

    def remote(src, dst, send, recv, ox, oy):
        return pltpu.make_async_remote_copy(
            src_ref=src, dst_ref=dst, send_sem=send, recv_sem=recv, device_id=(ox, oy), device_id_type=MESH
        )

    for d in range(1, ny):
        remote(row_out.at[y_at(d)], row_in.at[sy], small_send.at[0], small_recv.at[0], sx, y_at(d)).start()
    for g in range(staged):
        some = pl.ds(group(g), width)
        for d in range(1, ny):
            remote(tiles.at[some, y_at(d)], mid.at[some, sy], z_send.at[g], z_recv.at[g], sx, y_at(d)).start()
    row_in[pl.ds(sy, 1)] = row_out[pl.ds(sy, 1)]

    partners = ((x_at(nx - 1), sy), (x_at(1), sy), (sx, y_at(ny - 1)), (sx, y_at(1)))
    lane = lax.broadcasted_iota(jnp.int32, (8, LANES), 1)
    exists = [jnp.where(e, 1.0, 0.0).astype(F32) for e in (sx > 0, sx < nx - 1, sy > 0, sy < ny - 1)]

    def swap(n, field, planes):
        for q, plane in enumerate(planes):
            for t in range(nb):
                part = slice(t * LANES, (t + 1) * LANES)
                row_s[n, 0, q : q + 1, part] = field[plane + (t, slice(HALO, HALO + 1))]
                row_s[n, 1, q : q + 1, part] = field[plane + (t, slice(HALO + rows - 1, HALO + rows))]
        made = []
        for side, (ox, oy) in enumerate(partners):
            src = (row_s if side < 2 else col_s).at[n, side % 2]
            if side < 2:
                dst = row_r.at[n, 1 - side % 2]
            else:
                dst = cols_b.at[1 - side % 2] if n == 2 else col_r.at[n, 1 - side % 2]
            made.append(remote(src, dst, send_sem.at[n, side], recv_sem.at[n, side ^ 1], ox, oy))
        for copy in made:
            copy.start()

        def finish():
            for copy in made:
                copy.wait()
            for q, plane in enumerate(planes):
                for t in range(nb):
                    part = slice(t * LANES, (t + 1) * LANES)
                    field[plane + (t, slice(HALO - 1, HALO))] = row_r[n, 0, q : q + 1, part] * exists[0]
                    field[plane + (t, slice(HALO + rows, HALO + rows + 1))] = row_r[n, 1, q : q + 1, part] * exists[1]

        return finish

    pl.semaphore_wait(entered, ny - 1)

    def send_group(g):
        def send_tile(d, carry):
            ox = group(g) + lax.rem(sx + d // ny, width)
            oy = y_at(lax.rem(d, ny))
            remote(tiles.at[ox, oy], got.at[sx, sy], far_send, far_recv, ox, oy).start()
            return carry

        lax.fori_loop(0, width * ny, send_tile, 0)

    third = (groups - staged) // 3
    for g in range(staged, staged + third):
        send_group(g)

    for t in range(nb):
        loads[2 + t].wait()

    def pack_eta(i, carry):
        low = jnp.zeros((8, LANES), F32)
        high = jnp.zeros((8, LANES), F32)
        for k in range(layers):
            low = put(low, lane, k, eta[k, 0, at(i), :], 0)
            high = put(high, lane, k, eta[k, nb - 1, at(i), :], LANES - 1)
        col_s[0, 0, plain(i), :] = low
        col_s[0, 1, plain(i), :] = high
        return carry

    lax.fori_loop(0, blocks, pack_eta, 0)
    finish_eta = swap(0, eta, [(k,) for k in range(layers)])

    arrived = row_in.at[pl.ds(0, ny - 1)]
    pltpu.make_async_copy(arrived, arrived, small_recv.at[0]).wait()
    for y in range(ny):
        block[y : y + 1, :] = row_in[y]

    def send_block(d, carry):
        remote(block, anchors.at[sx], small_send.at[1], small_recv.at[1], x_at(d), sy).start()
        return carry

    lax.fori_loop(1, nx, send_block, 0)
    anchors[pl.ds(sx, 1)] = block[...].reshape((1,) + block.shape)

    kept.wait()
    for g in range(staged):
        if g > 0:
            for more in range(staged + third * g, groups if g == staged - 1 else staged + third * (g + 1)):
                send_group(more)
        bunch = mid.at[pl.ds(0, width), pl.ds(0, ny - 1)]
        pltpu.make_async_copy(bunch, bunch, z_recv.at[g]).wait()
        for j in range(width):
            ox = group(g) + lax.rem(sx + j, width)
            if g == 0 and j == 0:
                pltpu.make_async_copy(mid.at[sx], got.at[sx], own.at[1]).start()
            else:
                remote(mid.at[ox], got.at[sx], near_send, near_recv, ox, sy).start()

    finish_eta()
    loads[2 + nb].wait()

    def factor(i, carry):
        r = plain(i)
        last_up = [None] * nb
        last_ratio = [None] * nb
        centre = [eta[0, t, at(i), :] for t in range(nb)]
        for k in range(layers):
            low, high = shifts(nb, lane, centre, *halo_cols(col_r.at[0], i, k, exists[2:]))
            upper = [eta[k + 1, t, at(i), :] for t in range(nb)] if k < layers - 1 else None
            for t in range(nb):
                w = 0.5 * (centre[t] + eta[k, t, at(i, -1), :])
                e = 0.5 * (centre[t] + eta[k, t, at(i, 1), :])
                s = 0.5 * (centre[t] + low[t])
                n = 0.5 * (centre[t] + high[t])
                pivot = w + e + s + n
                if k == 0:
                    pivot = pivot + fric[r, t * LANES : (t + 1) * LANES]
                if k < layers - 1:
                    up = centre[t] + upper[t]
                    pivot = pivot + up
                if k > 0:
                    pivot = pivot + last_up[t] - last_up[t] * last_ratio[t]
                inverse = 1.0 / pivot
                west[k, t, r, :] = w * inverse
                east[k, t, r, :] = e * inverse
                south[k, t, r, :] = s * inverse
                north[k, t, r, :] = n * inverse
                if k > 0:
                    carry_c[k - 1, t, r, :] = last_up[t] * inverse
                if k < layers - 1:
                    last_ratio[t] = up * inverse
                    ratio_c[k, t, r, :] = last_ratio[t]
                    last_up[t] = up
                else:
                    top_c[t, r, :] = inverse
            centre = upper
        return carry

    lax.fori_loop(0, blocks, factor, 0)

    few = anchors.at[pl.ds(0, nx - 1)]
    pltpu.make_async_copy(few, few, small_recv.at[1]).wait()
    senders = nx * ny
    lookup[...] = jnp.transpose(anchors[...].astype(F32).reshape(senders, LANES))
    spot = lax.broadcasted_iota(jnp.int32, (nb * rows, senders), 0)
    band = jnp.zeros_like(spot)
    for t in range(1, nb):
        band = band + jnp.where(spot >= t * rows, 1, 0)
    spot = ((spot - band * rows) * nb + band).astype(F32)
    for load in loads[3 + nb :]:
        load.wait()
    far = got.at[pl.ds(0, (groups - staged) * width)]
    pltpu.make_async_copy(far, far, far_recv).wait()
    near = got.at[pl.ds(0, staged * width - 1)]
    pltpu.make_async_copy(near, near, near_recv).wait()
    pltpu.make_async_copy(mid.at[sx], got.at[sx], own.at[1]).wait()
    flat = got.reshape(senders * 3 * slots, LANES)
    for s in range(slots):
        row = lookup[pl.ds(s * nx + sx, 1), :]
        chosen = jnp.where(spot == row, 1.0, 0.0).astype(jnp.bfloat16)
        u, v, w = (flat[pl.ds(slots * c + s, senders, stride=3 * slots), :] for c in range(3))
        rest = jnp.concatenate([u * w, v * w, w], axis=1)
        for step in range(3):
            part = rest.astype(jnp.bfloat16)
            if step < 2:
                rest = rest - part.astype(F32)
            term = jnp.dot(chosen, part, preferred_element_type=F32)
            if s == 0 and step == 0:
                total[...] = term
            else:
                total[...] += term
    for t in range(nb):
        part = slice(t * LANES, (t + 1) * LANES)
        weight = total[t * rows : (t + 1) * rows, 2 * LANES : 3 * LANES]
        for c in range(2):
            rhs[c, t] = weight * vel[c, :, part] - total[t * rows : (t + 1) * rows, c * LANES : (c + 1) * LANES]

    icef = ice[0, 0].astype(F32)
    keep, gain = icef * (1.0 - RELAX), icef * RELAX
    planes = [(c, k) for c in range(2) for k in range(layers)]

    def first(i, carry):
        r = plain(i)
        low = jnp.zeros((8, LANES), F32)
        high = jnp.zeros((8, LANES), F32)
        for c in range(2):
            x = []
            for t in range(nb):
                top = rhs[c, t, r, :] * top_c[t, r, :]
                rhs[c, t, r, :] = top
                x.append(gain * top)
            for k in range(layers - 1, -1, -1):
                if k < layers - 1:
                    x = [ratio_c[k, t, r, :] * x[t] for t in range(nb)]
                for t in range(nb):
                    adj_a[c, k, t, at(i), :] = x[t]
                low = put(low, lane, c * layers + k, x[0], 0)
                high = put(high, lane, c * layers + k, x[nb - 1], LANES - 1)
        col_s[1, 0, r, :] = low
        col_s[1, 1, r, :] = high
        return carry

    lax.fori_loop(0, blocks, first, 0)
    swap(1, adj_a, planes)()

    def second(i, carry):
        edges = [jnp.zeros((8, LANES), F32), jnp.zeros((8, LANES), F32)]
        for c in range(2):
            def emit(k, made):
                for t in range(nb):
                    adj_b[c, k, t, at(i), :] = made[t]
                edges[0] = put(edges[0], lane, c * layers + k, made[0], 0)
                edges[1] = put(edges[1], lane, c * layers + k, made[nb - 1], LANES - 1)

            solve(i, c, lane, nb, adj_a, col_r.at[1], exists[2:], (west, east, south, north), carry_c, ratio_c, rhs, keep, gain, emit)
        col_s[2, 0, plain(i), :] = edges[0]
        col_s[2, 1, plain(i), :] = edges[1]
        return carry

    lax.fori_loop(0, blocks, second, 0)
    finish_b = swap(2, adj_b, planes)

    pltpu.make_async_copy(arrived, arrived, small_send.at[0]).wait()
    pltpu.make_async_copy(few, few, small_send.at[1]).wait()
    for g in range(staged):
        bunch = mid.at[pl.ds(0, width), pl.ds(0, ny - 1)]
        pltpu.make_async_copy(bunch, bunch, z_send.at[g]).wait()
    pltpu.make_async_copy(far, far, far_send).wait()
    pltpu.make_async_copy(near, near, near_send).wait()
    finish_b()


def last_sweep(pieces, ny, adj_b, west, east, south, north, carry_c, ratio_c, rhs, cols_b, velocity, ice,
               out, gradient, made_v, grad_v, vel, load_sem, store_sem):
    sy = lax.axis_index("gy")
    layers, nb, rows = west.shape[0], west.shape[1], west.shape[2]
    loads = [pltpu.make_async_copy(velocity.at[c, 0], vel.at[c], load_sem.at[c]) for c in range(2)]
    for load in loads:
        load.start()
    lane = lax.broadcasted_iota(jnp.int32, (8, LANES), 1)
    exists = [jnp.where(e, 1.0, 0.0).astype(F32) for e in (sy > 0, sy < ny - 1)]
    icef = ice[0, 0].astype(F32)
    keep, gain = icef * (1.0 - RELAX), icef * RELAX
    for load in loads:
        load.wait()

    def third(i, carry):
        r = plain(i)
        grad = [None] * nb
        for c in range(2):
            def emit(k, made):
                for t in range(nb):
                    part = slice(t * LANES, (t + 1) * LANES)
                    made_v[c, k, r, part] = made[t]
                    if k == 0:
                        term = made[t] * vel[c, r, part]
                        grad[t] = term if c == 0 else grad[t] + term

            solve(i, c, lane, nb, adj_b, cols_b, exists, (west, east, south, north), carry_c, ratio_c, rhs, keep, gain, emit)
        for t in range(nb):
            grad_v[r, t * LANES : (t + 1) * LANES] = -icef * grad[t]
        return carry

    blocks = rows // 8
    each = -(-blocks // pieces)
    stores = []
    for p in range(0, blocks, each):
        stop = min(p + each, blocks)
        lax.fori_loop(p, stop, third, 0)
        some = pl.ds(p * 8, (stop - p) * 8)
        stores.append(pltpu.make_async_copy(made_v.at[:, :, some, :], out.at[:, :, some, :], store_sem.at[len(stores)]))
        stores[-1].start()
    stores.append(pltpu.make_async_copy(grad_v, gradient, store_sem.at[len(stores)]))
    stores[-1].start()
    for store in stores:
        store.wait()


def per_device(nx, ny, velocity, viscosity, friction, ice_mask, obs_tiles, obs_cell, obs_count):
    comps, layers, rows, cols = velocity.shape
    slots, tile_len = obs_tiles.shape[4], obs_tiles.shape[6]
    nb = cols // tile_len
    width = max(1, nx // 8)
    staged, pieces = 2, 4
    in_vmem = pl.BlockSpec(memory_space=pltpu.VMEM)
    in_smem = pl.BlockSpec(memory_space=pltpu.SMEM)
    in_place = pl.BlockSpec(memory_space=pltpu.HBM)
    dma = pltpu.SemaphoreType.DMA

    tiles = obs_tiles.transpose(0, 1, 2, 3, 5, 4, 6).reshape(nx, ny, 3, slots, tile_len)
    cell = obs_cell.transpose(0, 1, 3, 4, 2).reshape(ny, slots, nx)
    count = obs_count.transpose(0, 1, 3, 2).reshape(ny, nx)
    halo_rows = rows + 2 * HALO
    packed = -(-comps * layers // 8) * 8
    face = pltpu.VMEM((layers, nb, rows, LANES), F32)
    link = pltpu.VMEM((layers - 1, nb, rows, LANES), F32)
    field = pltpu.VMEM((comps, layers, nb, halo_rows, LANES), F32)
    everyone = pltpu.VMEM((nx, ny, 3, slots, tile_len), F32)
    tiles, cell, count, velocity, viscosity, friction = (
        pltpu.with_memory_space_constraint(a, pltpu.HBM) for a in (tiles, cell, count, velocity, viscosity, friction)
    )
    state = pl.pallas_call(
        functools.partial(gather_and_sweep, nx, ny, width, staged),
        out_shape=(
            field, face, face, face, face, link, link,
            pltpu.VMEM((comps, nb, rows, LANES), F32),
            pltpu.VMEM((2, rows, LANES), F32),
        ),
        in_specs=[in_place] * 6 + [in_smem],
        out_specs=(in_vmem,) * 9,
        scratch_shapes=[
            pltpu.VMEM((layers, nb, halo_rows, LANES), F32),
            field,
            pltpu.VMEM((nb, rows, LANES), F32),
            pltpu.VMEM((comps, rows, cols), F32),
            pltpu.VMEM((rows, cols), F32),
            pltpu.VMEM((ny, slots, nx), jnp.int32),
            pltpu.VMEM((ny, nx), jnp.int32),
            everyone,
            everyone,
            pltpu.VMEM((ny, 1, LANES), jnp.int32),
            pltpu.VMEM((ny, 1, LANES), jnp.int32),
            pltpu.VMEM((ny, LANES), jnp.int32),
            pltpu.VMEM((nx, ny, LANES), jnp.int32),
            pltpu.VMEM((LANES, nx * ny), F32),
            pltpu.VMEM((nb * rows, 3 * LANES), F32),
            pltpu.VMEM((3, 2, packed, cols), F32),
            pltpu.VMEM((3, 2, packed, cols), F32),
            pltpu.VMEM((3, 2, rows, LANES), F32),
            pltpu.VMEM((2, 2, rows, LANES), F32),
            dma((nb + 5,)),
            dma((3, 4)),
            dma((3, 4)),
            pltpu.SemaphoreType.REGULAR,
            dma((staged,)),
            dma((staged,)),
            dma((2,)),
            dma, dma, dma, dma,
            dma((2,)),
            dma((2,)),
        ],
        compiler_params=pltpu.CompilerParams(collective_id=0, has_side_effects=True, vmem_limit_bytes=24 * 2**20),
        name="gather_and_sweep",
    )(tiles, cell, count, velocity, viscosity, friction, ice_mask)
    state = [pltpu.with_memory_space_constraint(a, pltpu.VMEM) for a in state]
    return pl.pallas_call(
        functools.partial(last_sweep, pieces, ny),
        out_shape=(
            jax.ShapeDtypeStruct(velocity.shape, F32),
            jax.ShapeDtypeStruct((rows, cols), F32),
        ),
        in_specs=[in_vmem] * 9 + [in_place, in_smem],
        out_specs=(in_place, in_place),
        scratch_shapes=[
            pltpu.VMEM((comps, layers, rows, cols), F32),
            pltpu.VMEM((rows, cols), F32),
            pltpu.VMEM((comps, rows, cols), F32),
            dma((2,)),
            dma((pieces + 1,)),
        ],
        compiler_params=pltpu.CompilerParams(vmem_limit_bytes=16 * 2**20),
        name="last_sweep",
    )(*state, velocity, ice_mask)


def solution(mesh):
    placed = (
        P(None, None, "gx", "gy"),
        P(None, "gx", "gy"),
        P("gx", "gy"),
        P("gx", "gy"),
        P("gx", "gy", None, None, None, None, None),
        P("gx", "gy", None, None, None),
        P("gx", "gy", None, None),
    )
    return jax.shard_map(
        functools.partial(per_device, mesh.shape["gx"], mesh.shape["gy"]),
        mesh=mesh,
        in_specs=placed,
        out_specs=(P(None, None, "gx", "gy"), P("gx", "gy")),
        check_vma=False,
    )
```

profile of v0, /device:TPU:1, one launch (start us, length us, event | category | flops | bytes accessed | tf_op | source)
XLA Modules:
  0.0 72.8 jit_solution(12622311222774577561)
XLA Ops:
  1.3 65.7 %gather_and_sweep.1 = (f32[2,10,3,112,128]{4,3,2,1,0:T(8,128)S(1)}, f32[10,3,96,128]{3,2,1,0:T(8,128)S(1)}, f32[10,3,96,128]{3,2,1,0:T(8,128)S(1)}, f32[10,3,96,...) custom-call(f32[32,8,3,4,128]{4,3,2,1,0:T(4,128)} %bitcast.9, ...), custom_call_target="tpu_custom_call" | custom-call | tf_op jit(solution)/shard_map/gather_and_sweep/pallas_call | solution.py:427
  67.0 5.9 %last_sweep.1 = (f32[2,10,96,384]{3,2,1,0:T(8,128)}, f32[96,384]{1,0:T(8,128)}) custom-call(f32[2,10,3,112,128]{4,3,2,1,0:T(8,128)S(1)} %get-tuple-element.11.adj_b, f32[10,3,96,128]{3,2,1,0:T(8,128)S(1)} %get-tuple-element.12.west, f32[10,3,96,128]{3,2,1,0:T(8,128)S(1)} %get-tuple-element.13.east, f32[10,3,96,128]{3,2,1,0:T(8,128)S(1)} %get-tuple-element.14.south, ...), custom_call_target="tpu_custom_call" | custom-call | tf_op jit(solution)/shard_map/last_sweep/pallas_call | solution.py:471
where the time goes:
time: 73 us; the launch traced here: 72.8 us
  Pallas kernels  71.6 us (98%)
  between operations  1.29 us (2%)
    pallas_call x1, Pallas kernels, per_device(): pl.pallas_call(functools.partial(gather_and_sweep, nx, ny, width, staged)...  65.7 us
    pallas_call x1, Pallas kernels, per_device(): pl.pallas_call(functools.partial(last_sweep, pieces, ny), out_shape=(jax....  5.87 us

commit v1 on v0

--- a/solution.py
+++ b/solution.py
@@ -14,11 +14,9 @@
 F32 = jnp.float32
 
 
-def shifts(nb, lane, values, low_halo, high_halo):
-    ups = [low_halo] + [pltpu.roll(a, 1, 1) for a in values]
-    downs = [pltpu.roll(a, LANES - 1, 1) for a in values] + [high_halo]
-    low = [jnp.where(lane == 0, ups[t], ups[t + 1]) for t in range(nb)]
-    high = [jnp.where(lane == LANES - 1, downs[t + 1], downs[t]) for t in range(nb)]
+def beside(lane, value, before, after):
+    low = pltpu.roll(jnp.where(lane == LANES - 1, before, value), 1, 1)
+    high = pltpu.roll(jnp.where(lane == 0, after, value), LANES - 1, 1)
     return low, high
 
 
@@ -30,43 +28,49 @@
     return pl.ds(pl.multiple_of(i * 8, 8), 8)
 
 
-def halo_cols(packed, i, q, exists):
-    lo = pltpu.roll(packed[0, plain(i), :], (LANES - q) % LANES, 1) * exists[0]
-    hi = pltpu.roll(packed[1, plain(i), :], LANES - 1 - q, 1) * exists[1]
-    return lo, hi
+def edge_tile(packed, side, i, q):
+    return pltpu.roll(packed[side, plain(i), :], (LANES - 1 - q if side == 0 else LANES - q) % LANES, 1)
 
 
 def put(packed, lane, q, value, edge):
     return jnp.where(lane == q, pltpu.roll(value, (q - edge) % LANES, 1), packed)
 
 
-def solve(i, c, lane, nb, old, cols, exists, faces, carry_c, ratio_c, rhs, keep, gain, emit):
+def solve(i, t, lane, nb, old, cols, faces, carry_c, ratio_c, rhs, keep, gain, emit):
     west, east, south, north = faces
-    layers, r = west.shape[0], plain(i)
-    forward = []
+    layers, r, both = west.shape[0], plain(i), range(2)
+    centre, forward = [], []
     for k in range(layers):
-        centre = [old[c, k, t, at(i), :] for t in range(nb)]
-        low, high = shifts(nb, lane, centre, *halo_cols(cols, i, c * layers + k, exists))
-        level = []
-        for t in range(nb):
-            value = west[k, t, r, :] * old[c, k, t, at(i, -1), :] + east[k, t, r, :] * old[c, k, t, at(i, 1), :]
-            value = value + (south[k, t, r, :] * low[t] + north[k, t, r, :] * high[t])
+        w, e, s, n = (face[k, t, r, :] for face in faces)
+        link = carry_c[k - 1, t, r, :] if k > 0 else None
+        here, level = [], []
+        for c in both:
+            a = old[c, k, t, at(i), :]
+            q = c * layers + k
+            before = old[c, k, t - 1, at(i), :] if t > 0 else edge_tile(cols, 0, i, q)
+            after = old[c, k, t + 1, at(i), :] if t < nb - 1 else edge_tile(cols, 1, i, q)
+            low, high = beside(lane, a, before, after)
+            value = (w * old[c, k, t, at(i, -1), :] + e * old[c, k, t, at(i, 1), :]) + (s * low + n * high)
             if k > 0:
-                value = value + carry_c[k - 1, t, r, :] * forward[k - 1][t]
+                value = value + link * forward[k - 1][c]
             if k == layers - 1:
                 value = value + rhs[c, t, r, :]
+            here.append(a)
             level.append(value)
+        centre.append(here)
         forward.append(level)
     x = forward[layers - 1]
     for k in range(layers - 1, -1, -1):
         if k < layers - 1:
-            x = [forward[k][t] + ratio_c[k, t, r, :] * x[t] for t in range(nb)]
-        emit(k, [keep * old[c, k, t, at(i), :] + gain * x[t] for t in range(nb)])
+            ratio = ratio_c[k, t, r, :]
+            x = [forward[k][c] + ratio * x[c] for c in both]
+        for c in both:
+            emit(c, k, keep * centre[k][c] + gain * x[c])
 
 
 def gather_and_sweep(nx, ny, width, staged, tiles, cell, count, velocity, viscosity, friction, ice,
                      adj_b, west, east, south, north, carry_c, ratio_c, rhs, cols_b,
-                     eta, adj_a, top_c, vel, fric, cell_v, count_v, mid, got, row_out, row_in, block, anchors, lookup, total,
+                     eta, adj_a, coef, top_c, vel, fric, cell_v, count_v, mid, got, row_out, row_in, block, anchors, lookup, total,
                      row_s, row_r, col_s, col_r,
                      load_sem, send_sem, recv_sem, entered, z_send, z_recv, own, far_send, far_recv, near_send, near_recv,
                      small_send, small_recv):
@@ -136,19 +140,20 @@
     lane = lax.broadcasted_iota(jnp.int32, (8, LANES), 1)
     exists = [jnp.where(e, 1.0, 0.0).astype(F32) for e in (sx > 0, sx < nx - 1, sy > 0, sy < ny - 1)]
 
-    def swap(n, field, planes):
-        for q, plane in enumerate(planes):
+    def swap(n, take):
+        count_q = len(take)
+        for q, rows_of in enumerate(take):
             for t in range(nb):
                 part = slice(t * LANES, (t + 1) * LANES)
-                row_s[n, 0, q : q + 1, part] = field[plane + (t, slice(HALO, HALO + 1))]
-                row_s[n, 1, q : q + 1, part] = field[plane + (t, slice(HALO + rows - 1, HALO + rows))]
+                row_s[n, 0, q : q + 1, part] = rows_of(t, 0)
+                row_s[n, 1, q : q + 1, part] = rows_of(t, rows - 1)
+        some = pl.ds(0, -(-count_q // 8) * 8)
         made = []
         for side, (ox, oy) in enumerate(partners):
-            src = (row_s if side < 2 else col_s).at[n, side % 2]
             if side < 2:
-                dst = row_r.at[n, 1 - side % 2]
+                src, dst = row_s.at[n, side % 2, some], row_r.at[n, 1 - side % 2, some]
             else:
-                dst = cols_b.at[1 - side % 2] if n == 2 else col_r.at[n, 1 - side % 2]
+                src, dst = col_s.at[n, side % 2], (cols_b.at[1 - side % 2] if n == 3 else col_r.at[n, 1 - side % 2])
             made.append(remote(src, dst, send_sem.at[n, side], recv_sem.at[n, side ^ 1], ox, oy))
         for copy in made:
             copy.start()
@@ -156,13 +161,35 @@
         def finish():
             for copy in made:
                 copy.wait()
+            for side in range(2):
+                if n == 3:
+                    cols_b[side] = cols_b[side] * exists[2 + side]
+                else:
+                    col_r[n, side] = col_r[n, side] * exists[2 + side]
+                row_r[n, side, some] = row_r[n, side, some] * exists[side]
+
+        return finish
+
+    def rows_in(field, plane):
+        return lambda t, r: field[plane + (t, slice(HALO + r, HALO + r + 1))]
+
+    def fill_rows(field, plane, values):
+        for side, r in ((0, HALO - 1), (1, HALO + rows)):
+            for t in range(nb):
+                field[plane + (t, slice(r, r + 1))] = values[side][:, t * LANES : (t + 1) * LANES]
+
+    def pack_cols(n, planes, tile_at):
+        def pack(i, carry):
+            low = jnp.zeros((8, LANES), F32)
+            high = jnp.zeros((8, LANES), F32)
             for q, plane in enumerate(planes):
-                for t in range(nb):
-                    part = slice(t * LANES, (t + 1) * LANES)
-                    field[plane + (t, slice(HALO - 1, HALO))] = row_r[n, 0, q : q + 1, part] * exists[0]
-                    field[plane + (t, slice(HALO + rows, HALO + rows + 1))] = row_r[n, 1, q : q + 1, part] * exists[1]
-
-        return finish
+                low = put(low, lane, q, tile_at(plane, 0, i), 0)
+                high = put(high, lane, q, tile_at(plane, nb - 1, i), LANES - 1)
+            col_s[n, 0, plain(i), :] = low
+            col_s[n, 1, plain(i), :] = high
+            return carry
+
+        lax.fori_loop(0, blocks, pack, 0)
 
     pl.semaphore_wait(entered, ny - 1)
 
@@ -182,18 +209,9 @@
     for t in range(nb):
         loads[2 + t].wait()
 
-    def pack_eta(i, carry):
-        low = jnp.zeros((8, LANES), F32)
-        high = jnp.zeros((8, LANES), F32)
-        for k in range(layers):
-            low = put(low, lane, k, eta[k, 0, at(i), :], 0)
-            high = put(high, lane, k, eta[k, nb - 1, at(i), :], LANES - 1)
-        col_s[0, 0, plain(i), :] = low
-        col_s[0, 1, plain(i), :] = high
-        return carry
-
-    lax.fori_loop(0, blocks, pack_eta, 0)
-    finish_eta = swap(0, eta, [(k,) for k in range(layers)])
+    single = [(k,) for k in range(layers)]
+    pack_cols(0, single, lambda plane, t, i: eta[plane + (t, at(i))])
+    finish_eta = swap(0, [rows_in(eta, plane) for plane in single])
 
     arrived = row_in.at[pl.ds(0, ny - 1)]
     pltpu.make_async_copy(arrived, arrived, small_recv.at[0]).wait()
@@ -222,46 +240,59 @@
                 remote(mid.at[ox], got.at[sx], near_send, near_recv, ox, sy).start()
 
     finish_eta()
+    for k in range(layers):
+        fill_rows(eta, (k,), [row_r[0, side, k : k + 1, :] for side in range(2)])
     loads[2 + nb].wait()
+    icef = ice[0, 0].astype(F32)
+    keep, gain = icef * (1.0 - RELAX), icef * RELAX
 
     def factor(i, carry):
         r = plain(i)
-        last_up = [None] * nb
-        last_ratio = [None] * nb
-        centre = [eta[0, t, at(i), :] for t in range(nb)]
-        for k in range(layers):
-            low, high = shifts(nb, lane, centre, *halo_cols(col_r.at[0], i, k, exists[2:]))
-            upper = [eta[k + 1, t, at(i), :] for t in range(nb)] if k < layers - 1 else None
-            for t in range(nb):
-                w = 0.5 * (centre[t] + eta[k, t, at(i, -1), :])
-                e = 0.5 * (centre[t] + eta[k, t, at(i, 1), :])
-                s = 0.5 * (centre[t] + low[t])
-                n = 0.5 * (centre[t] + high[t])
+        for t in range(nb):
+            last_up = last_ratio = None
+            ratios = []
+            for k in range(layers):
+                centre = eta[k, t, at(i), :]
+                before = eta[k, t - 1, at(i), :] if t > 0 else edge_tile(col_r.at[0], 0, i, k)
+                after = eta[k, t + 1, at(i), :] if t < nb - 1 else edge_tile(col_r.at[0], 1, i, k)
+                low, high = beside(lane, centre, before, after)
+                w = 0.5 * (centre + eta[k, t, at(i, -1), :])
+                e = 0.5 * (centre + eta[k, t, at(i, 1), :])
+                s = 0.5 * (centre + low)
+                n = 0.5 * (centre + high)
                 pivot = w + e + s + n
                 if k == 0:
                     pivot = pivot + fric[r, t * LANES : (t + 1) * LANES]
                 if k < layers - 1:
-                    up = centre[t] + upper[t]
+                    up = centre + eta[k + 1, t, at(i), :]
                     pivot = pivot + up
                 if k > 0:
-                    pivot = pivot + last_up[t] - last_up[t] * last_ratio[t]
+                    pivot = pivot + last_up - last_up * last_ratio
                 inverse = 1.0 / pivot
                 west[k, t, r, :] = w * inverse
                 east[k, t, r, :] = e * inverse
                 south[k, t, r, :] = s * inverse
                 north[k, t, r, :] = n * inverse
                 if k > 0:
-                    carry_c[k - 1, t, r, :] = last_up[t] * inverse
+                    carry_c[k - 1, t, r, :] = last_up * inverse
                 if k < layers - 1:
-                    last_ratio[t] = up * inverse
-                    ratio_c[k, t, r, :] = last_ratio[t]
-                    last_up[t] = up
+                    last_up, last_ratio = up, up * inverse
+                    ratio_c[k, t, r, :] = last_ratio
+                    ratios.append(last_ratio)
                 else:
                     top_c[t, r, :] = inverse
-            centre = upper
+                    unit = gain * inverse
+            for k in range(layers - 1, -1, -1):
+                if k < layers - 1:
+                    unit = ratios[k] * unit
+                coef[k, t, r, :] = unit
         return carry
 
     lax.fori_loop(0, blocks, factor, 0)
+
+    pack_cols(1, single, lambda plane, t, i: coef[plane + (t, plain(i))])
+    finish_coef = swap(1, [lambda t, r, k=k: coef[k, t, r : r + 1] for k in range(layers)])
+    finish_coef()
 
     few = anchors.at[pl.ds(0, nx - 1)]
     pltpu.make_async_copy(few, few, small_recv.at[1]).wait()
@@ -285,65 +316,71 @@
         chosen = jnp.where(spot == row, 1.0, 0.0).astype(jnp.bfloat16)
         u, v, w = (flat[pl.ds(slots * c + s, senders, stride=3 * slots), :] for c in range(3))
         rest = jnp.concatenate([u * w, v * w, w], axis=1)
-        for step in range(3):
-            part = rest.astype(jnp.bfloat16)
-            if step < 2:
-                rest = rest - part.astype(F32)
-            term = jnp.dot(chosen, part, preferred_element_type=F32)
-            if s == 0 and step == 0:
-                total[...] = term
-            else:
-                total[...] += term
+        high = rest.astype(jnp.bfloat16)
+        rest = rest - high.astype(F32)
+        middle = rest.astype(jnp.bfloat16)
+        parts = jnp.concatenate([high, middle, (rest - middle.astype(F32)).astype(jnp.bfloat16)], axis=0)
+        term = jnp.dot(jnp.concatenate([chosen] * 3, axis=1), parts, preferred_element_type=F32)
+        if s == 0:
+            total[...] = term
+        else:
+            total[...] += term
     for t in range(nb):
         part = slice(t * LANES, (t + 1) * LANES)
         weight = total[t * rows : (t + 1) * rows, 2 * LANES : 3 * LANES]
         for c in range(2):
             rhs[c, t] = weight * vel[c, :, part] - total[t * rows : (t + 1) * rows, c * LANES : (c + 1) * LANES]
 
-    icef = ice[0, 0].astype(F32)
-    keep, gain = icef * (1.0 - RELAX), icef * RELAX
-    planes = [(c, k) for c in range(2) for k in range(layers)]
+    pack_cols(2, [(c,) for c in range(2)], lambda plane, t, i: rhs[plane + (t, plain(i))])
+    finish_rhs = swap(2, [lambda t, r, c=c: rhs[c, t, r : r + 1] for c in range(2)])
 
     def first(i, carry):
         r = plain(i)
-        low = jnp.zeros((8, LANES), F32)
-        high = jnp.zeros((8, LANES), F32)
-        for c in range(2):
-            x = []
-            for t in range(nb):
-                top = rhs[c, t, r, :] * top_c[t, r, :]
-                rhs[c, t, r, :] = top
-                x.append(gain * top)
-            for k in range(layers - 1, -1, -1):
-                if k < layers - 1:
-                    x = [ratio_c[k, t, r, :] * x[t] for t in range(nb)]
-                for t in range(nb):
-                    adj_a[c, k, t, at(i), :] = x[t]
-                low = put(low, lane, c * layers + k, x[0], 0)
-                high = put(high, lane, c * layers + k, x[nb - 1], LANES - 1)
-        col_s[1, 0, r, :] = low
-        col_s[1, 1, r, :] = high
+        for t in range(nb):
+            drive = [rhs[c, t, r, :] for c in range(2)]
+            for k in range(layers):
+                unit = coef[k, t, r, :]
+                for c in range(2):
+                    adj_a[c, k, t, at(i), :] = unit * drive[c]
+            for c in range(2):
+                rhs[c, t, r, :] = drive[c] * top_c[t, r, :]
         return carry
 
     lax.fori_loop(0, blocks, first, 0)
-    swap(1, adj_a, planes)()
-
-    def second(i, carry):
-        edges = [jnp.zeros((8, LANES), F32), jnp.zeros((8, LANES), F32)]
-        for c in range(2):
-            def emit(k, made):
-                for t in range(nb):
-                    adj_b[c, k, t, at(i), :] = made[t]
-                edges[0] = put(edges[0], lane, c * layers + k, made[0], 0)
-                edges[1] = put(edges[1], lane, c * layers + k, made[nb - 1], LANES - 1)
-
-            solve(i, c, lane, nb, adj_a, col_r.at[1], exists[2:], (west, east, south, north), carry_c, ratio_c, rhs, keep, gain, emit)
-        col_s[2, 0, plain(i), :] = edges[0]
-        col_s[2, 1, plain(i), :] = edges[1]
+    finish_rhs()
+    for c in range(2):
+        edges = [row_r[1, side, 0 : -(-layers // 8) * 8, :] * row_r[2, side, c : c + 1, :] for side in range(2)]
+        for k in range(layers):
+            fill_rows(adj_a, (c, k), [edge[k : k + 1, :] for edge in edges])
+
+    def first_cols(i, carry):
+        for side in range(2):
+            unit = col_r[1, side, plain(i), :]
+            drive = col_r[2, side, plain(i), :]
+            unit = unit + pltpu.roll(unit, layers, 1)
+            col_r[2, side, plain(i), :] = unit * jnp.where(lane < layers, drive[:, 0:1], drive[:, 1:2])
         return carry
 
-    lax.fori_loop(0, blocks, second, 0)
-    finish_b = swap(2, adj_b, planes)
+    lax.fori_loop(0, blocks, first_cols, 0)
+
+    def second(tiles_done):
+        def sweep(i, carry):
+            for t in tiles_done:
+                def emit(c, k, made):
+                    adj_b[c, k, t, at(i), :] = made
+
+                solve(i, t, lane, nb, adj_a, col_r.at[2], (west, east, south, north), carry_c, ratio_c, rhs, keep, gain, emit)
+            return carry
+
+        return sweep
+
+    planes = [(c, k) for c in range(2) for k in range(layers)]
+    outer, inner = sorted({0, nb - 1}), list(range(1, nb - 1))
+    lax.fori_loop(0, blocks, second(outer), 0)
+    lax.fori_loop(0, 2, lambda i, carry: second(inner)(i * (blocks - 1), carry), 0)
+    pack_cols(3, planes, lambda plane, t, i: adj_b[plane + (t, at(i))])
+    finish_b = swap(3, [rows_in(adj_b, plane) for plane in planes])
+    lax.fori_loop(1, blocks - 1, second(inner), 0)
 
     pltpu.make_async_copy(arrived, arrived, small_send.at[0]).wait()
     pltpu.make_async_copy(few, few, small_send.at[1]).wait()
@@ -353,37 +390,27 @@
     pltpu.make_async_copy(far, far, far_send).wait()
     pltpu.make_async_copy(near, near, near_send).wait()
     finish_b()
-
-
-def last_sweep(pieces, ny, adj_b, west, east, south, north, carry_c, ratio_c, rhs, cols_b, velocity, ice,
+    for q, plane in enumerate(planes):
+        fill_rows(adj_b, plane, [row_r[3, side, q : q + 1, :] for side in range(2)])
+
+
+def last_sweep(pieces, adj_b, west, east, south, north, carry_c, ratio_c, rhs, cols_b, velocity, ice,
                out, gradient, made_v, grad_v, vel, load_sem, store_sem):
-    sy = lax.axis_index("gy")
     layers, nb, rows = west.shape[0], west.shape[1], west.shape[2]
     loads = [pltpu.make_async_copy(velocity.at[c, 0], vel.at[c], load_sem.at[c]) for c in range(2)]
     for load in loads:
         load.start()
     lane = lax.broadcasted_iota(jnp.int32, (8, LANES), 1)
-    exists = [jnp.where(e, 1.0, 0.0).astype(F32) for e in (sy > 0, sy < ny - 1)]
     icef = ice[0, 0].astype(F32)
     keep, gain = icef * (1.0 - RELAX), icef * RELAX
-    for load in loads:
-        load.wait()
 
     def third(i, carry):
         r = plain(i)
-        grad = [None] * nb
-        for c in range(2):
-            def emit(k, made):
-                for t in range(nb):
-                    part = slice(t * LANES, (t + 1) * LANES)
-                    made_v[c, k, r, part] = made[t]
-                    if k == 0:
-                        term = made[t] * vel[c, r, part]
-                        grad[t] = term if c == 0 else grad[t] + term
-
-            solve(i, c, lane, nb, adj_b, cols_b, exists, (west, east, south, north), carry_c, ratio_c, rhs, keep, gain, emit)
         for t in range(nb):
-            grad_v[r, t * LANES : (t + 1) * LANES] = -icef * grad[t]
+            def emit(c, k, made):
+                made_v[c, k, r, t * LANES : (t + 1) * LANES] = made
+
+            solve(i, t, lane, nb, adj_b, cols_b, (west, east, south, north), carry_c, ratio_c, rhs, keep, gain, emit)
         return carry
 
     blocks = rows // 8
@@ -395,6 +422,9 @@
         some = pl.ds(p * 8, (stop - p) * 8)
         stores.append(pltpu.make_async_copy(made_v.at[:, :, some, :], out.at[:, :, some, :], store_sem.at[len(stores)]))
         stores[-1].start()
+    for load in loads:
+        load.wait()
+    grad_v[...] = -icef * (made_v[0, 0] * vel[0] + made_v[1, 0] * vel[1])
     stores.append(pltpu.make_async_copy(grad_v, gradient, store_sem.at[len(stores)]))
     stores[-1].start()
     for store in stores:
@@ -406,7 +436,7 @@
     slots, tile_len = obs_tiles.shape[4], obs_tiles.shape[6]
     nb = cols // tile_len
     width = max(1, nx // 8)
-    staged, pieces = 2, 4
+    staged, pieces = 2, 6
     in_vmem = pl.BlockSpec(memory_space=pltpu.VMEM)
     in_smem = pl.BlockSpec(memory_space=pltpu.SMEM)
     in_place = pl.BlockSpec(memory_space=pltpu.HBM)
@@ -436,6 +466,7 @@
         scratch_shapes=[
             pltpu.VMEM((layers, nb, halo_rows, LANES), F32),
             field,
+            face,
             pltpu.VMEM((nb, rows, LANES), F32),
             pltpu.VMEM((comps, rows, cols), F32),
             pltpu.VMEM((rows, cols), F32),
@@ -449,13 +480,13 @@
             pltpu.VMEM((nx, ny, LANES), jnp.int32),
             pltpu.VMEM((LANES, nx * ny), F32),
             pltpu.VMEM((nb * rows, 3 * LANES), F32),
-            pltpu.VMEM((3, 2, packed, cols), F32),
-            pltpu.VMEM((3, 2, packed, cols), F32),
+            pltpu.VMEM((4, 2, packed, cols), F32),
+            pltpu.VMEM((4, 2, packed, cols), F32),
+            pltpu.VMEM((4, 2, rows, LANES), F32),
             pltpu.VMEM((3, 2, rows, LANES), F32),
-            pltpu.VMEM((2, 2, rows, LANES), F32),
             dma((nb + 5,)),
-            dma((3, 4)),
-            dma((3, 4)),
+            dma((4, 4)),
+            dma((4, 4)),
             pltpu.SemaphoreType.REGULAR,
             dma((staged,)),
             dma((staged,)),
@@ -469,7 +500,7 @@
     )(tiles, cell, count, velocity, viscosity, friction, ice_mask)
     state = [pltpu.with_memory_space_constraint(a, pltpu.VMEM) for a in state]
     return pl.pallas_call(
-        functools.partial(last_sweep, pieces, ny),
+        functools.partial(last_sweep, pieces),
         out_shape=(
             jax.ShapeDtypeStruct(velocity.shape, F32),
             jax.ShapeDtypeStruct((rows, cols), F32),

time: 73 us -> 72.3 us (level)
  Pallas kernels: 71.6 us -> 70.8 us
where the time goes in v1:
time: 72.3 us; the launch traced here: 72.1 us
  Pallas kernels  70.8 us (98%)
  between operations  1.29 us (2%)
    pallas_call x1, Pallas kernels, per_device(): pl.pallas_call(functools.partial(gather_and_sweep, nx, ny, width, staged)...  65.5 us
    pallas_call x1, Pallas kernels, per_device(): pl.pallas_call(functools.partial(last_sweep, pieces), out_shape=(jax.Shap...  5.26 us

profile of v1, /device:TPU:1, one launch (start us, length us, event | category | flops | bytes accessed | tf_op | source)
XLA Modules:
  0.0 72.1 jit_solution(6578125231136420127)
XLA Ops:
  1.3 65.5 %gather_and_sweep.1 = (f32[2,10,3,112,128]{4,3,2,1,0:T(8,128)S(1)}, f32[10,3,96,128]{3,2,1,0:T(8,128)S(1)}, f32[10,3,96,128]{3,2,1,0:T(8,128)S(1)}, f32[10,3,96,...) custom-call(f32[32,8,3,4,128]{4,3,2,1,0:T(4,128)} %bitcast.9, ...), custom_call_target="tpu_custom_call" | custom-call | tf_op jit(solution)/shard_map/gather_and_sweep/pallas_call | solution.py:457
  66.8 5.3 %last_sweep.1 = (f32[2,10,96,384]{3,2,1,0:T(8,128)}, f32[96,384]{1,0:T(8,128)}) custom-call(f32[2,10,3,112,128]{4,3,2,1,0:T(8,128)S(1)} %get-tuple-element.11.adj_b, f32[10,3,96,128]{3,2,1,0:T(8,128)S(1)} %get-tuple-element.12.west, f32[10,3,96,128]{3,2,1,0:T(8,128)S(1)} %get-tuple-element.13.east, f32[10,3,96,128]{3,2,1,0:T(8,128)S(1)} %get-tuple-element.14.south, ...), custom_call_target="tpu_custom_call" | custom-call | tf_op jit(solution)/shard_map/last_sweep/pallas_call | solution.py:502
